TPU v7x, 32 devices: a whole 2x2x4 slice. The times are simulated.
32 devices in a mesh: groups: 2 (over y), rows: 4 (over z), segment: 2 (over x), chan: 2 (over core).
Axes of the slice: x: 2, y: 2, z: 4, core: 2. Of those that a mesh axis runs over, the one named last changes fastest.
Arguments:
- latent: bfloat16 [8, 8, 160, 384], P(('groups', 'segment'), 'rows'), parts along dimension 0, may hold values from -6 to 6
- cache_mid: bfloat16 [4, 8, 160, 384], P('groups', 'rows'), parts along dimension 0, may hold values from -6 to 6
- cache_low: bfloat16 [4, 16, 320, 192], P('groups', 'rows'), parts along dimension 0, may hold values from -6 to 6
- gain_mid: float32 [384], replicated, may hold values from 0.1 to 1.9
- gain_attn: float32 [384], replicated, may hold values from 0.1 to 1.9
- gain_low: float32 [192], replicated, may hold values from 0.1 to 1.9
- conv_mid: bfloat16 [3, 3, 3, 384, 384], P(None, None, None, None, 'chan'), may hold values from -0.0625 to 0.0625
- attn_qkv: bfloat16 [384, 1152], replicated, may hold values from -4 to 4
- attn_proj: bfloat16 [384, 384], replicated, may hold values from -0.3125 to 0.3125
- conv_up: bfloat16 [3, 3, 384, 192], P(None, None, None, 'chan'), may hold values from -0.109375 to 0.109375
- conv_low: bfloat16 [3, 3, 3, 192, 192], P(None, None, None, None, 'chan'), may hold values from -0.078125 to 0.078125
Outputs:
- decoded: bfloat16 [8, 16, 320, 192], P(('groups', 'segment'), 'rows', None, 'chan'), parts along dimension 0
There are 2 independent parts, one for each index of `groups`. A program takes and returns all parts, laid end to end along the dimension named above; an argument that names none is the same for every part. Nothing has to cross between parts.
All inputs are finite; a program needn't handle non-finite values.
Results may differ from a plain program's by a relative error of at most 0.0071.
Values may be sent and summed in bfloat16 or wider, within the bound.
A program may use at most 128 MiB of HBM per device.

v0:
```python
import functools
import math

import jax
import jax.numpy as jnp
from jax import lax
from jax.experimental import pallas as pl
from jax.experimental.pallas import tpu as pltpu
from jax.sharding import PartitionSpec as P

MESH = pl.DeviceIdType.MESH
BF = jnp.bfloat16
F32 = jnp.float32


class Place:
    def __init__(self):
        self.rows, self.segs = lax.axis_size("rows"), lax.axis_size("segment")
        self.z, self.s, self.c = (lax.axis_index(a) for a in ("rows", "segment", "chan"))
        self.up, self.down = self.z > 0, self.z < self.rows - 1
        self.has_next, self.has_prev = self.s < self.segs - 1, self.s > 0

    def greet(self, wide, across):
        barrier = pltpu.get_barrier_semaphore()
        n = jnp.int32(1)
        pl.semaphore_signal(barrier, inc=1, device_id={"chan": 1 - self.c}, device_id_type=MESH)
        for ok, z in ((self.up, self.z - 1), (self.down, self.z + 1)):
            targets = [{"rows": z}]
            if wide:
                targets.append({"rows": z, "chan": 1 - self.c})
            for target in targets:

                @pl.when(ok)
                def _():
                    pl.semaphore_signal(barrier, inc=1, device_id=target, device_id_type=MESH)

            n = n + ok.astype(jnp.int32) * len(targets)
        if across:
            for ok, s in ((self.has_next, self.s + 1), (self.has_prev, self.s - 1)):

                @pl.when(ok)
                def _():
                    pl.semaphore_signal(barrier, inc=1, device_id={"segment": s}, device_id_type=MESH)

                n = n + ok.astype(jnp.int32)
        pl.semaphore_wait(barrier, n)


def remote(src, dst, send, recv, target):
    return pltpu.make_async_remote_copy(
        src_ref=src, dst_ref=dst, send_sem=send, recv_sem=recv, device_id=target, device_id_type=MESH
    )


class Spread:
    def __init__(self, here, src, buf, send, recv):
        c, z, last = here.c, here.z, buf.shape[0] - 1
        self.here = here
        self.partner = remote(src, buf.at[1 + c], send.at[0], recv.at[0], {"chan": 1 - c})
        self.low = [
            remote(src, buf.at[last], send.at[1 + k], recv.at[1], {"rows": z - 1, "chan": k}) for k in (0, 1)
        ]
        self.high = [
            remote(src, buf.at[0], send.at[1 + k], recv.at[2], {"rows": z + 1, "chan": k}) for k in (0, 1)
        ]

    def each(self, act):
        here = self.here

        @pl.when((here.c == 0) & here.up)
        def _():
            for copy in self.low:
                act(copy)

        @pl.when((here.c == 1) & here.down)
        def _():
            for copy in self.high:
                act(copy)

        act(self.partner)

    def start(self):
        self.each(lambda copy: copy.start())

    def wait_send(self):
        self.each(lambda copy: copy.wait_send())

    def wait_recv(self, when=True):
        here = self.here
        self.partner.wait_recv()

        @pl.when(here.down)
        def _():
            self.low[0].wait_recv()

        @pl.when(here.up)
        def _():
            self.high[0].wait_recv()


def normed(v, gain):
    return v * lax.rsqrt(jnp.mean(v * v, axis=-1, keepdims=True) + 1e-06) * gain


def silu(v):
    return v / (1.0 + jnp.exp(-v))


def stored_shifts(x, dst, width):
    n, ch = x.shape
    col = lax.broadcasted_iota(jnp.int32, (n, ch), 0)
    dst[:, :ch] = jnp.where(col == 0, 0.0, pltpu.roll(x, 1, 0)).astype(BF)
    dst[:, ch : 2 * ch] = x.astype(BF)
    dst[:, 2 * ch :] = jnp.where(col == n - 1, 0.0, pltpu.roll(x, n - 1, 0)).astype(BF)


def dot(a, b):
    return jnp.dot(a, b, preferred_element_type=F32)


def picker(rows, cols, hit):
    k = lax.broadcasted_iota(jnp.int32, (rows, cols), 0)
    n = lax.broadcasted_iota(jnp.int32, (rows, cols), 1)
    return jnp.where(hit(k, n), 1.0, 0.0).astype(BF)


def first_kernel(
    latent, cache, gain_mid, gain_attn, w, mine_out, attn_out,
    halo, prior, x3, acc, halfs, hs, hr, xs, xr, ps, pr, es, er, ls,
):
    here = Place()
    frames, rows, width, ch = latent.shape
    part = w.shape[-1]
    c, z = here.c, here.z
    here.greet(True, True)
    to_up = remote(latent.at[:, 0], halo.at[1], hs.at[0], hr.at[0], {"rows": z - 1})
    to_down = remote(latent.at[:, rows - 1], halo.at[0], hs.at[1], hr.at[1], {"rows": z + 1})
    across = remote(latent.at[:, c], prior.at[1 + c], xs, xr, {"segment": here.s + 1})
    local = pltpu.make_async_copy(cache.at[:, c], prior.at[1 + c], ls)
    spread = Spread(here, prior.at[1 + c], prior, ps, pr)

    pl.when(here.has_next)(lambda: across.start())
    pl.when(here.up)(lambda: to_up.start())
    pl.when(here.down)(lambda: to_down.start())

    @pl.when(jnp.logical_not(here.has_prev))
    def _():
        local.start()
        local.wait()

    gain = gain_mid[...]

    def fill(slot, row, x, active):
        v = x.astype(F32)
        if active:
            v = silu(normed(v, gain))
        stored_shifts(v, x3.at[slot, row], width)

    for f in range(frames):
        for r in range(rows):
            fill(frames + f, 1 + r, latent[f, r], True)

    @pl.when(here.has_prev)
    def _():
        across.wait_recv()

    spread.start()
    for ok, copy, k in ((here.up, to_down, 0), (here.down, to_up, 1)):
        row = 0 if k == 0 else rows + 1

        @pl.when(ok)
        def _():
            copy.wait_recv()
            for f in range(frames):
                fill(frames + f, row, halo[k, f], True)

        @pl.when(jnp.logical_not(ok))
        def _():
            for f in range(frames):
                x3[frames + f, row] = jnp.zeros((width, 3 * ch), BF)

    pick = picker(ch, part, lambda k, n: k == n + c * part)
    acc[...] = dot(latent[...].reshape(-1, ch), pick)

    def tap(kt, kh):
        x = x3[pl.ds(kt, frames), pl.ds(kh, rows)].reshape(frames * rows * width, 3 * ch)
        acc[...] += dot(x, w[kt, kh])

    taps_t, taps_h = w.shape[:2]
    lax.fori_loop(0, taps_h, lambda i, _: (tap(taps_t - 1, i), 0)[1], 0)
    spread.wait_recv()
    for row in range(rows + 2):
        inside = True if 0 < row <= rows else (here.up if row == 0 else here.down)
        known = jnp.logical_and(here.z >= 0, inside)
        for active in (False, True):
            origin = here.has_prev if active else jnp.logical_not(here.has_prev)

            @pl.when(known & origin)
            def _():
                for f in range(frames):
                    fill(f, row, prior[row, f], active)

        if row in (0, rows + 1):

            @pl.when(jnp.logical_not(inside))
            def _():
                for f in range(frames):
                    x3[f, row] = jnp.zeros((width, 3 * ch), BF)

    def rest(i, _):
        tap(i // taps_h, i % taps_h)
        return 0

    lax.fori_loop(0, (taps_t - 1) * taps_h, rest, 0)
    result = acc[...].astype(BF).reshape(frames, rows, width, part)
    halfs[0] = jnp.where(c == 0, result[:, 1].astype(F32), result[:, 0].astype(F32)).astype(BF)
    swap = remote(halfs.at[0], halfs.at[1], es, er, {"chan": 1 - c})
    swap.start()
    kept = jnp.where(c == 0, result[:, 0].astype(F32), result[:, 1].astype(F32)).astype(BF)
    put = [picker(part, ch, lambda k, n: n == k + off * part) for off in (c, 1 - c)]
    full = dot(kept.reshape(-1, part), put[0])
    swap.wait()
    full = full + dot(halfs[1].reshape(-1, part), put[1])
    mine_out[...] = full.astype(BF).reshape(frames, width, ch)
    attn_out[...] = normed(full, gain_attn[...]).astype(BF).reshape(frames, width, ch)
    spread.wait_send()
    pl.when(here.has_next)(lambda: across.wait_send())
    pl.when(here.up)(lambda: to_up.wait_send())
    pl.when(here.down)(lambda: to_down.wait_send())


def attn_kernel(mine, attn_in, wqkv, wproj, out, every, scores, values, query, send, recv):
    here = Place()
    frames, width, ch = attn_in.shape
    z, c, chips = here.z, here.c, here.rows
    here.greet(False, False)

    def copy(src, row, f, kind, target):
        return remote(src, every.at[row, f], send.at[row, f, kind], recv.at[row, f], target)

    links = ((0, here.down, {"rows": z + 1}), (1, here.up, {"rows": z - 1}))
    partner = {"chan": 1 - c}
    own = 2 * z + c
    for f in range(frames):
        for kind, ok, target in links:
            pl.when(ok)(lambda: copy(attn_in.at[f], own, f, kind, target).start())
        copy(attn_in.at[f], own, f, 2, partner).start()

    scale = 1.0 / math.sqrt(ch)

    def process(row, f, x):
        kv = dot(x, wqkv[:, ch:]).astype(BF)
        values[row, f] = kv[:, ch:]
        scores[row, f] = (
            lax.dot_general(query[f], kv[:, :ch], (((1,), (1,)), ((), ())), preferred_element_type=F32) * scale
        )

    for f in range(frames):
        query[f] = dot(attn_in[f], wqkv[:, :ch]).astype(BF)
        process(own, f, attn_in[f])

    def other(row, f):
        copy(attn_in.at[f], row, f, 2, partner).wait_recv()
        process(row, f, every[row, f])

    for f in range(frames):
        other(2 * z + 1 - c, f)

    def hop(k, _):
        sides = ((z - k, z - k >= 0, links[0]), (z + k, z + k < chips, links[1]))
        for f in range(frames):
            for src, valid, (kind, ok, target) in sides:
                row = 2 * src + c

                @pl.when(valid)
                def _():
                    copy(attn_in.at[f], row, f, kind, target).wait_recv()
                    copy(every.at[row, f], row, f, 2, partner).start()

                    @pl.when(ok)
                    def _():
                        copy(every.at[row, f], row, f, kind, target).start()

        for src, valid, _ in sides:

            @pl.when(valid)
            def _():
                for f in range(frames):
                    process(2 * src + c, f, every[2 * src + c, f])
                for f in range(frames):
                    other(2 * src + 1 - c, f)

        return 0

    lax.fori_loop(1, chips, hop, 0)

    for f in range(frames):
        part = scores[:, f]
        top = jnp.max(jnp.max(part, axis=0), axis=-1, keepdims=True)
        e = jnp.exp(part - top[None])
        total = jnp.sum(jnp.sum(e, axis=0), axis=-1, keepdims=True)
        weights = (e / total[None]).astype(BF)
        mixed = jnp.zeros((width, ch), F32)
        for row in range(2 * chips):
            mixed = mixed + dot(weights[row], values[row, f])
        out[f] = (mine[f].astype(F32) + dot(mixed.astype(BF), wproj[...])).astype(BF)

    for f in range(frames):
        for kind, ok, target in links:
            pl.when(ok)(lambda: copy(attn_in.at[f], own, f, kind, target).wait_send())
        copy(attn_in.at[f], own, f, 2, partner).wait_send()

    def drain(k, _):
        for f in range(frames):
            for src, valid, (kind, ok, target) in (
                (z - k, z - k >= 0, links[0]),
                (z + k, z + k < chips, links[1]),
            ):
                row = 2 * src + c

                @pl.when(valid)
                def _():
                    copy(every.at[row, f], row, f, 2, partner).wait_send()

                    @pl.when(ok)
                    def _():
                        copy(every.at[row, f], row, f, kind, target).wait_send()

        return 0

    lax.fori_loop(1, chips, drain, 0)


def last_kernel(
    second, cache, gain, wup, wlow, out,
    own, prior, chalo, wother, wmix, wtap, grid, x, upper, acc, ss, sr, xs, xr, ps, pr, cs, cr, ws, wr, ls,
):
    here = Place()
    frames, width, ch = second.shape
    c, z = here.c, here.z
    tall = cache.shape[1]
    two = cache.shape[-1]
    low = two // 2
    part = wup.shape[-1]
    first = jnp.logical_not(here.has_prev)
    here.greet(True, True)
    across = remote(second, prior.at[1 + c], xs, xr, {"segment": here.s + 1})
    local = pltpu.make_async_copy(second, own.at[1 + c], ls)
    spread = Spread(here, second, own, ss, sr)
    relay = Spread(here, prior.at[1 + c], prior, ps, pr)
    to_up = remote(cache.at[:, 0], chalo.at[1], cs.at[0], cr.at[0], {"rows": z - 1})
    to_down = remote(cache.at[:, tall - 1], chalo.at[0], cs.at[1], cr.at[1], {"rows": z + 1})
    weights = remote(wup, wother, ws, wr, {"chan": 1 - c})

    pl.when(here.has_next)(lambda: across.start())
    spread.start()
    weights.start()
    local.start()
    pl.when(first & here.up)(lambda: to_up.start())
    pl.when(first & here.down)(lambda: to_down.start())

    taps_t, taps_h = wlow.shape[:2]

    def lay(i, _):
        kt, kh = i // taps_h, i % taps_h
        tap = [wlow[kt, kh, k * low : (k + 1) * low] for k in range(3)]
        none = jnp.zeros((low, part), BF)
        blocks = ((tap[1], tap[0]), (tap[2], tap[1]), (none, tap[2]), (tap[0], none))
        for at, (even, odd) in enumerate(blocks):
            wtap[kt, kh, at * low : (at + 1) * low, :] = jnp.concatenate([even, odd], axis=1)
        return 0

    lax.fori_loop(0, taps_t * taps_h, lay, 0)

    weights.wait_recv()
    swap = c == 1
    for kh in range(3):
        full = []
        for kw in range(3):
            a, b = wup[kh, kw].astype(F32), wother[kh, kw].astype(F32)
            full.append(jnp.concatenate([jnp.where(swap, b, a), jnp.where(swap, a, b)], axis=1))
        for at, (even, odd) in enumerate(((1, 1), (2, 0), (0, 2))):
            wmix[kh, at] = jnp.concatenate([full[even], full[odd]], axis=1).astype(BF)

    for edge, inside in ((0, here.up), (own.shape[0] - 1, here.down)):

        @pl.when(jnp.logical_not(inside))
        def _():
            own[edge] = jnp.zeros(own.shape[1:], BF)
            prior[edge] = jnp.zeros(own.shape[1:], BF)

    local.wait()
    spread.wait_recv()

    @pl.when(here.has_prev)
    def _():
        across.wait_recv()
        relay.start()

    gains = gain[...]
    lane = lax.broadcasted_iota(jnp.int32, (width, two), 1)
    col = lax.broadcasted_iota(jnp.int32, (width, two), 0)
    evens = lane < low

    def spaced(v, keep_first, keep_last):
        v_next = jnp.where(col == width - 1, 0.0, pltpu.roll(v, width - 1, 0))
        v_prev = jnp.where(col == 0, 0.0, pltpu.roll(v, 1, 0))
        return jnp.where(evens, keep_first(v_prev, v_next), keep_last(v_prev, v_next))

    def put(slot, row, v):
        x[slot, row, :, :two] = v.astype(BF)
        x[slot, row, :, two:] = spaced(v, lambda p, n: n, lambda p, n: p).astype(BF)

    height = own.shape[0]

    def raise_frame(tile, f, slot, keep):
        flat = tile[:, f].reshape(height * width, ch)
        for kh in range(3):
            grid[kh, :, :, :two] = (dot(flat, wmix[kh, 0]) + dot(flat, wmix[kh, 1])).reshape(height, width, two)
            grid[kh, :, :, two:] = dot(flat, wmix[kh, 2]).reshape(height, width, two)
        for r in range(tall + 2):
            i, odd = (r + 1) // 2, (r + 1) % 2
            sources = (i, i, i + 1) if odd else (i - 1, i, i)
            both = sum(grid[kh, sources[kh]] for kh in range(3))
            v = both[:, :two] + spaced(both[:, two:], lambda p, n: p, lambda p, n: n)
            v = v.astype(BF)
            if keep and 0 < r <= tall:
                upper[f, r - 1] = v
            v = v.astype(F32)
            sq = v * v
            mean_even = jnp.sum(jnp.where(evens, sq, 0.0), axis=-1, keepdims=True) / low
            mean_odd = jnp.sum(jnp.where(evens, 0.0, sq), axis=-1, keepdims=True) / low
            v = v * jnp.where(evens, lax.rsqrt(mean_even + 1e-06), lax.rsqrt(mean_odd + 1e-06)) * gains
            v = silu(v)
            if r == 0:
                v = jnp.where(here.up, v, 0.0)
            if r == tall + 1:
                v = jnp.where(here.down, v, 0.0)
            put(slot, r, v.astype(BF).astype(F32))

    lax.fori_loop(0, frames, lambda f, _: (raise_frame(own, f, frames + f, True), 0)[1], 0)

    n = 2 * part
    pick = picker(two, n, lambda k, j: k == jnp.where(j < part, j, j - part + low) + c * part)
    acc[...] = dot(upper[...].reshape(-1, two), pick)

    def tap(kt, kh):
        v = x[pl.ds(kt, frames), pl.ds(kh, tall)].reshape(frames * tall * width, 2 * two)
        acc[...] += dot(v, wtap[kt, kh])

    lax.fori_loop(0, taps_h, lambda i, _: (tap(taps_t - 1, i), 0)[1], 0)

    @pl.when(here.has_prev)
    def _():
        relay.wait_recv()
        lax.fori_loop(0, frames, lambda f, _: (raise_frame(prior, f, f, False), 0)[1], 0)

    @pl.when(first)
    def _():
        def take(i, _):
            put(i // tall, 1 + i % tall, cache[i // tall, i % tall].astype(F32))
            return 0

        lax.fori_loop(0, frames * tall, take, 0)

    for row, inside, k, copy in ((0, here.up, 0, to_down), (tall + 1, here.down, 1, to_up)):

        @pl.when(first & inside)
        def _():
            copy.wait_recv()
            for f in range(frames):
                put(f, row, chalo[k, f].astype(F32))

        @pl.when(first & jnp.logical_not(inside))
        def _():
            for f in range(frames):
                put(f, row, jnp.zeros((width, two), F32))

    def rest(i, _):
        tap(i // taps_h, i % taps_h)
        return 0

    lax.fori_loop(0, (taps_t - 1) * taps_h, rest, 0)
    out[...] = acc[...].astype(BF).reshape(out.shape)
    spread.wait_send()
    weights.wait_send()
    pl.when(here.has_prev)(lambda: relay.wait_send())
    pl.when(here.has_next)(lambda: across.wait_send())
    pl.when(first & here.up)(lambda: to_up.wait_send())
    pl.when(first & here.down)(lambda: to_down.wait_send())


def call(kernel, number, outs, scratch, *args):
    return pl.pallas_call(
        kernel,
        out_shape=outs,
        in_specs=[pl.BlockSpec(memory_space=pltpu.VMEM)] * len(args),
        out_specs=jax.tree.map(lambda _: pl.BlockSpec(memory_space=pltpu.VMEM), outs),
        scratch_shapes=scratch,
        compiler_params=pltpu.CompilerParams(
            collective_id=number, has_side_effects=True, vmem_limit_bytes=60 * 1024 * 1024
        ),
    )(*args)


def body(
    latent, cache_mid, cache_low, gain_mid, gain_attn, gain_low, conv_mid, attn_qkv, attn_proj, conv_up, conv_low
):
    frames, rows, width, ch = latent.shape
    part = conv_mid.shape[-1]
    dma, one = pltpu.SemaphoreType.DMA, pltpu.SemaphoreType.DMA(())
    row = jax.ShapeDtypeStruct((frames, width, ch), BF)
    taps_t, taps_h, taps_w = conv_mid.shape[:3]
    mine, attn_in = call(
        first_kernel,
        0,
        (row, row),
        [
            pltpu.VMEM((2, frames, width, ch), BF),
            pltpu.VMEM((rows + 2, frames, width, ch), BF),
            pltpu.VMEM((2 * frames, rows + 2, width, taps_w * ch), BF),
            pltpu.VMEM((frames * rows * width, part), F32),
            pltpu.VMEM((2, frames, width, part), BF),
            dma((2,)), dma((2,)), one, one, dma((3,)), dma((3,)), one, one, one,
        ],
        latent,
        cache_mid,
        gain_mid.reshape(1, -1),
        gain_attn.reshape(1, -1),
        conv_mid.reshape(taps_t, taps_h, taps_w * ch, part),
    )
    total = rows * lax.axis_size("rows")
    second = call(
        attn_kernel,
        1,
        row,
        [
            pltpu.VMEM((total, frames, width, ch), BF),
            pltpu.VMEM((total, frames, width, width), F32),
            pltpu.VMEM((total, frames, width, ch), BF),
            pltpu.VMEM((frames, width, ch), BF),
            dma((total, frames, 3)),
            dma((total, frames)),
        ],
        mine,
        attn_in,
        attn_qkv,
        attn_proj,
    )
    _, tall, wide, low = cache_low.shape
    cut = conv_low.shape[-1]
    two = 2 * low
    taps_t, taps_h, taps_w = conv_low.shape[:3]
    decoded = call(
        last_kernel,
        2,
        jax.ShapeDtypeStruct((frames, tall, width, 2 * cut), BF),
        [
            pltpu.VMEM((rows + 2, frames, width, ch), BF),
            pltpu.VMEM((rows + 2, frames, width, ch), BF),
            pltpu.VMEM((2, frames, width, two), BF),
            pltpu.VMEM(conv_up.shape, BF),
            pltpu.VMEM((3, 3, ch, two), BF),
            pltpu.VMEM((taps_t, taps_h, 2 * two, 2 * cut), BF),
            pltpu.VMEM((3, rows + 2, width, 2 * two), F32),
            pltpu.VMEM((2 * frames, tall + 2, width, 2 * two), BF),
            pltpu.VMEM((frames, tall, width, two), BF),
            pltpu.VMEM((frames * tall * width, 2 * cut), F32),
            dma((3,)), dma((3,)), one, one, dma((3,)), dma((3,)), dma((2,)), dma((2,)), one, one, one,
        ],
        second,
        cache_low.reshape(frames, tall, width, two),
        jnp.concatenate([gain_low, gain_low]).reshape(1, -1),
        conv_up,
        conv_low.reshape(taps_t, taps_h, taps_w * low, cut),
    )
    return decoded.reshape(frames, tall, wide, cut)


def solution(mesh):
    placed = (
        P(("groups", "segment"), "rows", None, None),
        P("groups", "rows", None, None),
        P("groups", "rows", None, None),
        P(),
        P(),
        P(),
        P(None, None, None, None, "chan"),
        P(),
        P(),
        P(None, None, None, "chan"),
        P(None, None, None, None, "chan"),
    )
    return jax.shard_map(
        body,
        mesh=mesh,
        in_specs=placed,
        out_specs=P(("groups", "segment"), "rows", None, "chan"),
        check_vma=False,
    )
```

profile of v0, /device:TPU:2, one launch (start us, length us, event | category | flops | bytes accessed | tf_op | source)
XLA Modules:
  0.0 103.0 jit_solution(16672022934109511623)
XLA Ops:
  0.0 0.0 copy-start.2
  0.0 0.0 copy-start.3
  0.0 8.2 %copy.16 = bf16[3,3,3,384,192]{4,3,2,1,0:T(8,128)(2,1)} copy(bf16[3,3,3,384,192]{3,4,2,1,0:T(8,128)(2,1)} %param.17) | data formatting | bytes 7962624 | tf_op args[6]
  8.2 0.0 copy-done.2
  8.2 0.6 reshape.21.gain_mid
  8.7 0.0 copy-done.3
  8.8 0.6 reshape.22.gain_attn
  9.3 26.5 %shard_map.109 = (bf16[2,160,384]{2,1,0:T(8,128)(2,1)}, bf16[2,160,384]{2,1,0:T(8,128)(2,1)}) custom-call(bf16[2,2,160,384]{3,2,1,0:T(8,128)(2,1)} %latent.1, bf16[2,2,160,384]{3,2,1,0:T(8,128)(2,1)} %cache.1, f32[1,384]{1,0:T(1,128)} %reshape.21.gain_mid, f32[1,384]{1,0:T(1,128)} %reshape.22.gain_attn, bf16[3,3,1152,192]{3,2,1,0:T(8,128)(2,1)} %bitcast.6), custom_call_target="tpu_custom_call" | custom-call | tf_op jit(solution)/shard_map/pallas_call | solution.py:494
  35.8 0.0 copy-start
  35.8 25.5 %shard_map.110.second = bf16[2,160,384]{2,1,0:T(8,128)(2,1)} custom-call(bf16[2,160,384]{2,1,0:T(8,128)(2,1)} %get-tuple-element.7.mine, bf16[2,160,384]{2,1,0:T(8,128)(2,1)} %get-tuple-element.8.attn_in, bf16[384,1152]{1,0:T(8,128)(2,1)} %wqkv.1, bf16[384,384]{1,0:T(8,128)(2,1)} %wproj.1), custom_call_target="tpu_custom_call" | custom-call | tf_op jit(solution)/shard_map/pallas_call | solution.py:494
  61.3 0.0 copy-done
  61.3 0.7 copy.17
  62.0 0.0 copy-start.1
  62.0 1.6 %reshape.24.cache = bf16[2,4,160,384]{3,2,1,0:T(8,128)(2,1)} reshape(bf16[2,4,320,192]{3,2,1,0:T(8,128)(2,1)S(1)} %copy.17) | data formatting | bytes 1966080 | tf_op jit(solution)/shard_map/reshape | solution.py:572
  63.7 0.0 copy-done.1
  63.7 0.0 copy-start.4
  63.7 1.3 %copy.18.wup = bf16[3,3,384,96]{3,2,1,0:T(8,128)(2,1)} copy(bf16[3,3,384,96]{2,3,1,0:T(8,128)(2,1)S(1)} %copy-done.1) | data formatting | bytes 1327104 | tf_op args[9]
  64.9 0.0 copy-done.4
  64.9 0.1 pad_maximum_fusion
  65.0 0.6 reshape.25.gain
  65.6 34.8 %shard_map.111 = bf16[2,4,160,192]{3,2,1,0:T(8,128)(2,1)} custom-call(bf16[2,160,384]{2,1,0:T(8,128)(2,1)} %shard_map.110.second, bf16[2,4,160,384]{3,2,1,0:T(8,128)(2,1)} %reshape.24.cache, f32[1,384]{1,0:T(1,128)} %reshape.25.gain, bf16[3,3,384,96]{3,2,1,0:T(8,128)(2,1)} %copy.18.wup, bf16[3,3,576,96]{3,2,1,0:T(8,128)(2,1)} %bitcast.7), custom_call_target="tpu_custom_call" | custom-call | tf_op jit(solution)/shard_map/pallas_call | solution.py:494
  100.3 1.6 %reshape.27 = bf16[2,4,320,96]{3,2,1,0:T(8,128)(2,1)S(1)} reshape(bf16[2,4,160,192]{3,2,1,0:T(8,128)(2,1)} %shard_map.111) | data formatting | bytes 983040 | tf_op jit(solution)/shard_map/reshape | solution.py:577
  101.9 1.1 %copy.19 = bf16[2,4,320,96]{2,3,1,0:T(8,128)(2,1)} copy(bf16[2,4,320,96]{3,2,1,0:T(8,128)(2,1)S(1)} %reshape.27) | data formatting | bytes 983040 | tf_op jit(solution)/shard_map/reshape | solution.py:577
Async XLA Ops:
  0.0 8.2 %copy-start.2 = (f32[384]{0:T(512)S(1)}, f32[384]{0:T(512)}, u32[]{:S(2)}) copy-start(f32[384]{0:T(512)} %param.14) | copy-start | bytes 4612
  0.0 8.7 %copy-start.3 = (f32[384]{0:T(512)S(1)}, f32[384]{0:T(512)}, u32[]{:S(2)}) copy-start(f32[384]{0:T(512)} %param.15) | copy-start | bytes 4612
  35.8 25.5 %copy-start = (bf16[2,4,320,192]{2,3,1,0:T(8,128)(2,1)S(1)}, bf16[2,4,320,192]{2,3,1,0:T(8,128)(2,1)}, u32[]{:S(2)}) copy-start(bf16[2,4,320,192]{2,3,1,0:T(8,128)(2,1)} %param.13) | copy-start | bytes 2949124
  62.0 1.6 %copy-start.1 = (bf16[3,3,384,96]{2,3,1,0:T(8,128)(2,1)S(1)}, bf16[3,3,384,96]{2,3,1,0:T(8,128)(2,1)}, u32[]{:S(2)}) copy-start(bf16[3,3,384,96]{2,3,1,0:T(8,128)(2,1)} %param.20) | copy-start | bytes 1990660
  63.7 1.3 %copy-start.4 = (f32[192]{0:T(256)S(1)}, f32[192]{0:T(256)}, u32[]{:S(2)}) copy-start(f32[192]{0:T(256)} %param.16) | copy-start | bytes 2308
where the time goes:
time: 104 us; the launch traced here: 103 us
  Pallas kernels  86.7 us (83%)
  local copies, waits for them, and re-layouts  16.2 us (16%)
    pallas_call x3, Pallas kernels, call(): pl.pallas_call(kernel, out_shape=outs, in_specs=[pl.BlockSpec(memory_spac...  86.7 us
    unnamed x13, local copies, waits for them, and re-layouts  10.2 us
    reshape x2, local copies, waits for them, and re-layouts, body(): return decoded.reshape(frames, tall, wide, cut)  2.66 us

commit v1 on v0

--- a/solution.py
+++ b/solution.py
@@ -103,7 +103,7 @@
 
 
 def silu(v):
-    return v / (1.0 + jnp.exp(-v))
+    return 0.5 * v * (1.0 + jnp.tanh(0.5 * v))
 
 
 def stored_shifts(x, dst, width):
@@ -118,6 +118,10 @@
     return jnp.dot(a, b, preferred_element_type=F32)
 
 
+def dot_t(a, b):
+    return lax.dot_general(a, b, (((1,), (1,)), ((), ())), preferred_element_type=F32)
+
+
 def picker(rows, cols, hit):
     k = lax.broadcasted_iota(jnp.int32, (rows, cols), 0)
     n = lax.broadcasted_iota(jnp.int32, (rows, cols), 1)
@@ -125,13 +129,15 @@
 
 
 def first_kernel(
-    latent, cache, gain_mid, gain_attn, w, mine_out, attn_out,
-    halo, prior, x3, acc, halfs, hs, hr, xs, xr, ps, pr, es, er, ls,
+    latent, cache, gain_mid, gain_attn, w_hbm, mine_out, attn_out,
+    w, halo, prior, x3, acc, halfs, hs, hr, xs, xr, ps, pr, es, er, ls, wsem,
 ):
     here = Place()
     frames, rows, width, ch = latent.shape
-    part = w.shape[-1]
+    part = w.shape[-2]
     c, z = here.c, here.z
+    fetch = pltpu.make_async_copy(w_hbm, w, wsem)
+    fetch.start()
     here.greet(True, True)
     to_up = remote(latent.at[:, 0], halo.at[1], hs.at[0], hr.at[0], {"rows": z - 1})
     to_down = remote(latent.at[:, rows - 1], halo.at[0], hs.at[1], hr.at[1], {"rows": z + 1})
@@ -148,7 +154,7 @@
         local.start()
         local.wait()
 
-    gain = gain_mid[...]
+    gain = gain_mid[...].reshape(1, ch)
 
     def fill(slot, row, x, active):
         v = x.astype(F32)
@@ -184,9 +190,10 @@
 
     def tap(kt, kh):
         x = x3[pl.ds(kt, frames), pl.ds(kh, rows)].reshape(frames * rows * width, 3 * ch)
-        acc[...] += dot(x, w[kt, kh])
+        acc[...] += sum(dot_t(x[:, k * ch : (k + 1) * ch], w[kt, kh, k]) for k in range(3))
 
     taps_t, taps_h = w.shape[:2]
+    fetch.wait()
     lax.fori_loop(0, taps_h, lambda i, _: (tap(taps_t - 1, i), 0)[1], 0)
     spread.wait_recv()
     for row in range(rows + 2):
@@ -222,7 +229,7 @@
     swap.wait()
     full = full + dot(halfs[1].reshape(-1, part), put[1])
     mine_out[...] = full.astype(BF).reshape(frames, width, ch)
-    attn_out[...] = normed(full, gain_attn[...]).astype(BF).reshape(frames, width, ch)
+    attn_out[...] = normed(full, gain_attn[...].reshape(1, ch)).astype(BF).reshape(frames, width, ch)
     spread.wait_send()
     pl.when(here.has_next)(lambda: across.wait_send())
     pl.when(here.up)(lambda: to_up.wait_send())
@@ -331,35 +338,90 @@
     lax.fori_loop(1, chips, drain, 0)
 
 
+class Deal:
+    def __init__(self, here, src, buf, send, recv):
+        c, z, last = here.c, here.z, buf.shape[0] - 1
+        self.here = here
+        self.local = pltpu.make_async_copy(src.at[c], buf.at[1 + c], send.at[3])
+        self.partner = remote(src.at[1 - c], buf.at[1 + c], send.at[0], recv.at[0], {"chan": 1 - c})
+        self.low = [
+            remote(src.at[k], buf.at[last], send.at[1 + k], recv.at[1], {"rows": z - 1, "chan": k}) for k in (0, 1)
+        ]
+        self.high = [
+            remote(src.at[k], buf.at[0], send.at[1 + k], recv.at[2], {"rows": z + 1, "chan": k}) for k in (0, 1)
+        ]
+
+    def each(self, act):
+        here = self.here
+
+        @pl.when((here.c == 0) & here.up)
+        def _():
+            for copy in self.low:
+                act(copy)
+
+        @pl.when((here.c == 1) & here.down)
+        def _():
+            for copy in self.high:
+                act(copy)
+
+        act(self.partner)
+
+    def start(self):
+        self.each(lambda copy: copy.start())
+        self.local.start()
+
+    def wait_send(self):
+        self.each(lambda copy: copy.wait_send())
+
+    def wait_recv(self):
+        here = self.here
+        self.local.wait()
+        self.partner.wait_recv()
+        pl.when(here.down)(lambda: self.low[0].wait_recv())
+        pl.when(here.up)(lambda: self.high[0].wait_recv())
+
+
 def last_kernel(
-    second, cache, gain, wup, wlow, out,
-    own, prior, chalo, wother, wmix, wtap, grid, x, upper, acc, ss, sr, xs, xr, ps, pr, cs, cr, ws, wr, ls,
+    second, cache, gain, wup, wlow_hbm, out,
+    wlow, own, stage, prior, chalo, wfull, wmix, wtap, grid, x, upper, acc,
+    ss, sr, xs, xr, ps, pr, cs, cr, ws, wr, ls, fs, es, er, us, ur,
 ):
     here = Place()
     frames, width, ch = second.shape
     c, z = here.c, here.z
     tall = cache.shape[1]
-    two = cache.shape[-1]
-    low = two // 2
-    part = wup.shape[-1]
+    low = cache.shape[2]
+    wide = cache.shape[3]
+    two = 2 * low
+    part = wup.shape[2]
     first = jnp.logical_not(here.has_prev)
+    fetch = pltpu.make_async_copy(wlow_hbm, wlow, fs)
+    fetch.start()
+    local = pltpu.make_async_copy(wup, wfull.at[c], ls)
+    local.start()
     here.greet(True, True)
-    across = remote(second, prior.at[1 + c], xs, xr, {"segment": here.s + 1})
-    local = pltpu.make_async_copy(second, own.at[1 + c], ls)
-    spread = Spread(here, second, own, ss, sr)
-    relay = Spread(here, prior.at[1 + c], prior, ps, pr)
+    across = remote(second, stage, xs, xr, {"segment": here.s + 1})
+    spread = Deal(here, second, own, ss, sr)
+    relay = Deal(here, stage, prior, ps, pr)
     to_up = remote(cache.at[:, 0], chalo.at[1], cs.at[0], cr.at[0], {"rows": z - 1})
     to_down = remote(cache.at[:, tall - 1], chalo.at[0], cs.at[1], cr.at[1], {"rows": z + 1})
-    weights = remote(wup, wother, ws, wr, {"chan": 1 - c})
+    weights = remote(wup, wfull.at[c], ws, wr, {"chan": 1 - c})
 
     pl.when(here.has_next)(lambda: across.start())
     spread.start()
     weights.start()
-    local.start()
     pl.when(first & here.up)(lambda: to_up.start())
     pl.when(first & here.down)(lambda: to_down.start())
 
+    for edge, inside in ((0, here.up), (own.shape[0] - 1, here.down)):
+
+        @pl.when(jnp.logical_not(inside))
+        def _():
+            own[edge] = jnp.zeros(own.shape[1:], BF)
+            prior[edge] = jnp.zeros(own.shape[1:], BF)
+
     taps_t, taps_h = wlow.shape[:2]
+    fetch.wait()
 
     def lay(i, _):
         kt, kh = i // taps_h, i % taps_h
@@ -372,24 +434,15 @@
 
     lax.fori_loop(0, taps_t * taps_h, lay, 0)
 
+    local.wait()
     weights.wait_recv()
-    swap = c == 1
     for kh in range(3):
-        full = []
-        for kw in range(3):
-            a, b = wup[kh, kw].astype(F32), wother[kh, kw].astype(F32)
-            full.append(jnp.concatenate([jnp.where(swap, b, a), jnp.where(swap, a, b)], axis=1))
-        for at, (even, odd) in enumerate(((1, 1), (2, 0), (0, 2))):
-            wmix[kh, at] = jnp.concatenate([full[even], full[odd]], axis=1).astype(BF)
-
-    for edge, inside in ((0, here.up), (own.shape[0] - 1, here.down)):
-
-        @pl.when(jnp.logical_not(inside))
-        def _():
-            own[edge] = jnp.zeros(own.shape[1:], BF)
-            prior[edge] = jnp.zeros(own.shape[1:], BF)
-
-    local.wait()
+        for at, sides in enumerate(((1, 1), (2, 0), (0, 2))):
+            for side, kw in enumerate(sides):
+                for half in (0, 1):
+                    start = side * low + half * part
+                    wmix[kh, at, start : start + part] = wfull[half, kh, kw]
+
     spread.wait_recv()
 
     @pl.when(here.has_prev)
@@ -397,7 +450,8 @@
         across.wait_recv()
         relay.start()
 
-    gains = gain[...]
+    gains = gain[...].reshape(1, low)
+    gains = jnp.concatenate([gains, gains], axis=1)
     lane = lax.broadcasted_iota(jnp.int32, (width, two), 1)
     col = lax.broadcasted_iota(jnp.int32, (width, two), 0)
     evens = lane < low
@@ -407,25 +461,40 @@
         v_prev = jnp.where(col == 0, 0.0, pltpu.roll(v, 1, 0))
         return jnp.where(evens, keep_first(v_prev, v_next), keep_last(v_prev, v_next))
 
+    def beside(slot, row, v):
+        x[slot, row, :, two:] = spaced(v, lambda p, n: n, lambda p, n: p).astype(BF)
+
     def put(slot, row, v):
         x[slot, row, :, :two] = v.astype(BF)
-        x[slot, row, :, two:] = spaced(v, lambda p, n: n, lambda p, n: p).astype(BF)
+        beside(slot, row, v)
 
     height = own.shape[0]
 
-    def raise_frame(tile, f, slot, keep):
-        flat = tile[:, f].reshape(height * width, ch)
+    def row_copy(slot, at, r):
+        piece = x.at[slot, r, :, pl.ds(0, two)]
+        return remote(piece, piece, es.at[at, r], er.at[at, r], {"chan": 1 - c})
+
+    def upper_copy(f, r):
+        return remote(upper.at[f, r], upper.at[f, r], us.at[r], ur.at[r], {"chan": 1 - c})
+
+    def raise_frame(tile, at):
+        slot = at * frames + c
         for kh in range(3):
-            grid[kh, :, :, :two] = (dot(flat, wmix[kh, 0]) + dot(flat, wmix[kh, 1])).reshape(height, width, two)
-            grid[kh, :, :, two:] = dot(flat, wmix[kh, 2]).reshape(height, width, two)
+            n0, n1 = (0, height - 1) if kh == 0 else (0, height) if kh == 1 else (1, height)
+            flat = tile[n0:n1].reshape((n1 - n0) * width, ch)
+            grid[kh, n0:n1, :, :two] = (dot_t(flat, wmix[kh, 0]) + dot_t(flat, wmix[kh, 1])).reshape(
+                n1 - n0, width, two
+            )
+            grid[kh, n0:n1, :, two:] = dot_t(flat, wmix[kh, 2]).reshape(n1 - n0, width, two)
         for r in range(tall + 2):
             i, odd = (r + 1) // 2, (r + 1) % 2
             sources = (i, i, i + 1) if odd else (i - 1, i, i)
             both = sum(grid[kh, sources[kh]] for kh in range(3))
             v = both[:, :two] + spaced(both[:, two:], lambda p, n: p, lambda p, n: n)
             v = v.astype(BF)
-            if keep and 0 < r <= tall:
-                upper[f, r - 1] = v
+            if at and 0 < r <= tall:
+                upper[c, r - 1] = v
+                upper_copy(c, r - 1).start()
             v = v.astype(F32)
             sq = v * v
             mean_even = jnp.sum(jnp.where(evens, sq, 0.0), axis=-1, keepdims=True) / low
@@ -436,13 +505,15 @@
                 v = jnp.where(here.up, v, 0.0)
             if r == tall + 1:
                 v = jnp.where(here.down, v, 0.0)
-            put(slot, r, v.astype(BF).astype(F32))
-
-    lax.fori_loop(0, frames, lambda f, _: (raise_frame(own, f, frames + f, True), 0)[1], 0)
-
-    n = 2 * part
-    pick = picker(two, n, lambda k, j: k == jnp.where(j < part, j, j - part + low) + c * part)
-    acc[...] = dot(upper[...].reshape(-1, two), pick)
+            put(slot, r, v)
+            row_copy(slot, at, r).start()
+        other = at * frames + 1 - c
+        for r in range(tall + 2):
+            row_copy(other, at, r).wait_recv()
+            beside(other, r, x[other, r, :, :two].astype(F32))
+
+    raise_frame(own, 1)
+    acc[...] = jnp.zeros(acc.shape, F32)
 
     def tap(kt, kh):
         v = x[pl.ds(kt, frames), pl.ds(kh, tall)].reshape(frames * tall * width, 2 * two)
@@ -453,15 +524,20 @@
     @pl.when(here.has_prev)
     def _():
         relay.wait_recv()
-        lax.fori_loop(0, frames, lambda f, _: (raise_frame(prior, f, f, False), 0)[1], 0)
+        raise_frame(prior, 0)
+
+    spots = [picker(width, wide, lambda k, n: n == 2 * k + p) for p in (0, 1)]
+
+    def take(slot, row, flipped):
+        put(slot, row, jnp.concatenate([dot_t(spot, flipped) for spot in spots], axis=1))
 
     @pl.when(first)
     def _():
-        def take(i, _):
-            put(i // tall, 1 + i % tall, cache[i // tall, i % tall].astype(F32))
+        def each(i, _):
+            take(i // tall, 1 + i % tall, cache[i // tall, i % tall])
             return 0
 
-        lax.fori_loop(0, frames * tall, take, 0)
+        lax.fori_loop(0, frames * tall, each, 0)
 
     for row, inside, k, copy in ((0, here.up, 0, to_down), (tall + 1, here.down, 1, to_up)):
 
@@ -469,7 +545,7 @@
         def _():
             copy.wait_recv()
             for f in range(frames):
-                put(f, row, chalo[k, f].astype(F32))
+                take(f, row, chalo[k, f])
 
         @pl.when(first & jnp.logical_not(inside))
         def _():
@@ -481,20 +557,41 @@
         return 0
 
     lax.fori_loop(0, (taps_t - 1) * taps_h, rest, 0)
-    out[...] = acc[...].astype(BF).reshape(out.shape)
+    n = 2 * part
+    pick = picker(two, n, lambda k, j: k == jnp.where(j < part, j, j - part + low) + c * part)
+    for r in range(tall):
+        upper_copy(1 - c, r).wait_recv()
+    acc[...] += dot(upper[...].reshape(-1, two), pick)
+
+    def finish(i, _):
+        done = acc[pl.ds(pl.multiple_of(i * width, width), width), :].T.astype(BF)
+        out[i // tall, i % tall] = (dot(done[:part], spots[0]) + dot(done[part:], spots[1])).astype(BF)
+        return 0
+
+    lax.fori_loop(0, frames * tall, finish, 0)
     spread.wait_send()
     weights.wait_send()
-    pl.when(here.has_prev)(lambda: relay.wait_send())
+    for r in range(tall):
+        upper_copy(c, r).wait_send()
+    for r in range(tall + 2):
+        row_copy(frames + c, 1, r).wait_send()
+
+    @pl.when(here.has_prev)
+    def _():
+        relay.wait_send()
+        for r in range(tall + 2):
+            row_copy(c, 0, r).wait_send()
+
     pl.when(here.has_next)(lambda: across.wait_send())
     pl.when(first & here.up)(lambda: to_up.wait_send())
     pl.when(first & here.down)(lambda: to_down.wait_send())
 
 
-def call(kernel, number, outs, scratch, *args):
+def call(kernel, number, outs, scratch, *args, far=()):
     return pl.pallas_call(
         kernel,
         out_shape=outs,
-        in_specs=[pl.BlockSpec(memory_space=pltpu.VMEM)] * len(args),
+        in_specs=[pl.BlockSpec(memory_space=pl.ANY if i in far else pltpu.VMEM) for i in range(len(args))],
         out_specs=jax.tree.map(lambda _: pl.BlockSpec(memory_space=pltpu.VMEM), outs),
         scratch_shapes=scratch,
         compiler_params=pltpu.CompilerParams(
@@ -516,18 +613,20 @@
         0,
         (row, row),
         [
+            pltpu.VMEM((taps_t, taps_h, taps_w, part, ch), BF),
             pltpu.VMEM((2, frames, width, ch), BF),
             pltpu.VMEM((rows + 2, frames, width, ch), BF),
             pltpu.VMEM((2 * frames, rows + 2, width, taps_w * ch), BF),
             pltpu.VMEM((frames * rows * width, part), F32),
             pltpu.VMEM((2, frames, width, part), BF),
-            dma((2,)), dma((2,)), one, one, dma((3,)), dma((3,)), one, one, one,
+            dma((2,)), dma((2,)), one, one, dma((3,)), dma((3,)), one, one, one, one,
         ],
         latent,
         cache_mid,
-        gain_mid.reshape(1, -1),
-        gain_attn.reshape(1, -1),
-        conv_mid.reshape(taps_t, taps_h, taps_w * ch, part),
+        gain_mid,
+        gain_attn,
+        jnp.swapaxes(conv_mid, 3, 4),
+        far=(4,),
     )
     total = rows * lax.axis_size("rows")
     second = call(
@@ -554,27 +653,31 @@
     decoded = call(
         last_kernel,
         2,
-        jax.ShapeDtypeStruct((frames, tall, width, 2 * cut), BF),
+        jax.ShapeDtypeStruct((frames, tall, cut, wide), BF),
         [
-            pltpu.VMEM((rows + 2, frames, width, ch), BF),
-            pltpu.VMEM((rows + 2, frames, width, ch), BF),
-            pltpu.VMEM((2, frames, width, two), BF),
-            pltpu.VMEM(conv_up.shape, BF),
-            pltpu.VMEM((3, 3, ch, two), BF),
+            pltpu.VMEM((taps_t, taps_h, taps_w * low, cut), BF),
+            pltpu.VMEM((rows + 2, width, ch), BF),
+            pltpu.VMEM((frames, width, ch), BF),
+            pltpu.VMEM((rows + 2, width, ch), BF),
+            pltpu.VMEM((2, frames, low, wide), BF),
+            pltpu.VMEM((2, 3, 3, cut, ch), BF),
+            pltpu.VMEM((3, 3, two, ch), BF),
             pltpu.VMEM((taps_t, taps_h, 2 * two, 2 * cut), BF),
             pltpu.VMEM((3, rows + 2, width, 2 * two), F32),
             pltpu.VMEM((2 * frames, tall + 2, width, 2 * two), BF),
             pltpu.VMEM((frames, tall, width, two), BF),
             pltpu.VMEM((frames * tall * width, 2 * cut), F32),
-            dma((3,)), dma((3,)), one, one, dma((3,)), dma((3,)), dma((2,)), dma((2,)), one, one, one,
+            dma((4,)), dma((3,)), one, one, dma((4,)), dma((3,)), dma((2,)), dma((2,)), one, one, one, one,
+            dma((2, tall + 2)), dma((2, tall + 2)), dma((tall,)), dma((tall,)),
         ],
         second,
-        cache_low.reshape(frames, tall, width, two),
-        jnp.concatenate([gain_low, gain_low]).reshape(1, -1),
-        conv_up,
+        jnp.swapaxes(cache_low, 2, 3),
+        gain_low,
+        jnp.swapaxes(conv_up, 2, 3),
         conv_low.reshape(taps_t, taps_h, taps_w * low, cut),
+        far=(4,),
     )
-    return decoded.reshape(frames, tall, wide, cut)
+    return jnp.swapaxes(decoded, 2, 3)
 
 
 def solution(mesh):

time: 104 us -> 83.6 us (0.80)
  local copies, waits for them, and re-layouts: 16.2 us -> 1.94 us
  Pallas kernels: 86.7 us -> 81.4 us
    unnamed x13 -> x1, local copies, waits for them, and re-layouts: 10.2 us -> 1.94 us
    reshape x6 -> x0, local copies, waits for them, and re-layouts: 6 us -> none  [the longest x2 2.66 us: body(): return decoded.reshape(frames, tall, wide, cut)]
    pallas_call x3, Pallas kernels: 86.7 us -> 81.4 us  [call(): pl.pallas_call(kernel, out_shape=outs, in_specs=[pl.BlockSpec(memory_spac...]
where the time goes in v1:
time: 83.6 us; the launch traced here: 83.3 us
  Pallas kernels  81.4 us (97%)
  local copies, waits for them, and re-layouts  1.94 us (2%)
    pallas_call x3, Pallas kernels, call(): pl.pallas_call(kernel, out_shape=outs, in_specs=[pl.BlockSpec(memory_spac...  81.4 us
    unnamed x1, local copies, waits for them, and re-layouts  1.94 us

profile of v1, /device:TPU:2, one launch (start us, length us, event | category | flops | bytes accessed | tf_op | source)
XLA Modules:
  0.0 83.3 jit_solution(2633478625854536797)
XLA Ops:
  0.0 25.2 %shard_map.109 = (bf16[2,160,384]{2,1,0:T(8,128)(2,1)}, bf16[2,160,384]{2,1,0:T(8,128)(2,1)}) custom-call(bf16[2,2,160,384]{3,2,1,0:T(8,128)(2,1)} %latent.1, bf16[2,2,160,384]{3,2,1,0:T(8,128)(2,1)} %cache.1, f32[384]{0:T(512)} %gain_mid.1, f32[384]{0:T(512)} %gain_attn.1, bf16[3,3,3,192,384]{4,3,2,1,0:T(8,128)(2,1)} %bitcast.5), custom_call_target="tpu_custom_call" | custom-call | tf_op jit(solution)/shard_map/pallas_call | solution.py:591
  25.2 25.3 %shard_map.110.second = bf16[2,160,384]{2,1,0:T(8,128)(2,1)} custom-call(bf16[2,160,384]{2,1,0:T(8,128)(2,1)} %get-tuple-element.7.mine, bf16[2,160,384]{2,1,0:T(8,128)(2,1)} %get-tuple-element.8.attn_in, bf16[384,1152]{1,0:T(8,128)(2,1)} %wqkv.1, bf16[384,384]{1,0:T(8,128)(2,1)} %wproj.1), custom_call_target="tpu_custom_call" | custom-call | tf_op jit(solution)/shard_map/pallas_call | solution.py:591
  50.5 30.9 %shard_map.111 = bf16[2,4,96,320]{3,2,1,0:T(8,128)(2,1)} custom-call(bf16[2,160,384]{2,1,0:T(8,128)(2,1)} %shard_map.110.second, bf16[2,4,192,320]{3,2,1,0:T(8,128)(2,1)} %bitcast.8, f32[192]{0:T(256)} %gain.1, bf16[3,3,96,384]{3,2,1,0:T(8,128)(2,1)} %bitcast.9, bf16[3,3,576,96]{3,2,1,0:T(8,128)(2,1)} %bitcast.7), custom_call_target="tpu_custom_call" | custom-call | tf_op jit(solution)/shard_map/pallas_call | solution.py:591
  81.4 1.9 %copy.13 = bf16[2,4,320,96]{2,3,1,0:T(8,128)(2,1)} copy(bf16[2,4,320,96]{2,3,1,0:T(8,128)(2,1)} %bitcast.6) | data formatting | bytes 983040

commit v2 on v1

--- a/solution.py
+++ b/solution.py
@@ -106,12 +106,12 @@
     return 0.5 * v * (1.0 + jnp.tanh(0.5 * v))
 
 
-def stored_shifts(x, dst, width):
+def stored_shifts(x, dst, row, rows):
     n, ch = x.shape
     col = lax.broadcasted_iota(jnp.int32, (n, ch), 0)
-    dst[:, :ch] = jnp.where(col == 0, 0.0, pltpu.roll(x, 1, 0)).astype(BF)
-    dst[:, ch : 2 * ch] = x.astype(BF)
-    dst[:, 2 * ch :] = jnp.where(col == n - 1, 0.0, pltpu.roll(x, n - 1, 0)).astype(BF)
+    dst[row] = jnp.where(col == 0, 0.0, pltpu.roll(x, 1, 0)).astype(BF)
+    dst[rows + row] = x.astype(BF)
+    dst[2 * rows + row] = jnp.where(col == n - 1, 0.0, pltpu.roll(x, n - 1, 0)).astype(BF)
 
 
 def dot(a, b):
@@ -120,6 +120,14 @@
 
 def dot_t(a, b):
     return lax.dot_general(a, b, (((1,), (1,)), ((), ())), preferred_element_type=F32)
+
+
+def run_taps(tap, taps_t, taps_h, frames, own):
+    for back in range(taps_t):
+        split = min(back, frames)
+        low, high = (split, frames) if own else (0, split)
+        if low < high:
+            lax.fori_loop(0, taps_h, lambda i, _: (tap(taps_t - 1 - back, i, low, high), 0)[1], 0)
 
 
 def picker(rows, cols, hit):
@@ -128,17 +136,15 @@
     return jnp.where(hit(k, n), 1.0, 0.0).astype(BF)
 
 
-def first_kernel(
-    latent, cache, gain_mid, gain_attn, w_hbm, mine_out, attn_out,
-    w, halo, prior, x3, acc, halfs, hs, hr, xs, xr, ps, pr, es, er, ls, wsem,
+def first_part(
+    here, latent, cache, gain_mid, gain_attn, w_hbm, mine_out, attn_out,
+    w, halo, prior, halfs, hs, hr, xs, xr, ps, pr, es, er, ls, wsem, begun, x3, acc,
 ):
-    here = Place()
     frames, rows, width, ch = latent.shape
     part = w.shape[-2]
     c, z = here.c, here.z
     fetch = pltpu.make_async_copy(w_hbm, w, wsem)
     fetch.start()
-    here.greet(True, True)
     to_up = remote(latent.at[:, 0], halo.at[1], hs.at[0], hr.at[0], {"rows": z - 1})
     to_down = remote(latent.at[:, rows - 1], halo.at[0], hs.at[1], hr.at[1], {"rows": z + 1})
     across = remote(latent.at[:, c], prior.at[1 + c], xs, xr, {"segment": here.s + 1})
@@ -154,13 +160,14 @@
         local.start()
         local.wait()
 
+    begun()
     gain = gain_mid[...].reshape(1, ch)
 
     def fill(slot, row, x, active):
         v = x.astype(F32)
         if active:
             v = silu(normed(v, gain))
-        stored_shifts(v, x3.at[slot, row], width)
+        stored_shifts(v, x3.at[slot], row, rows + 2)
 
     for f in range(frames):
         for r in range(rows):
@@ -183,18 +190,23 @@
         @pl.when(jnp.logical_not(ok))
         def _():
             for f in range(frames):
-                x3[frames + f, row] = jnp.zeros((width, 3 * ch), BF)
+                for k in range(3):
+                    x3[frames + f, k * (rows + 2) + row] = jnp.zeros((width, ch), BF)
 
     pick = picker(ch, part, lambda k, n: k == n + c * part)
-    acc[...] = dot(latent[...].reshape(-1, ch), pick)
-
-    def tap(kt, kh):
-        x = x3[pl.ds(kt, frames), pl.ds(kh, rows)].reshape(frames * rows * width, 3 * ch)
-        acc[...] += sum(dot_t(x[:, k * ch : (k + 1) * ch], w[kt, kh, k]) for k in range(3))
+    acc[: frames * rows * width, :part] = dot(latent[...].reshape(-1, ch), pick)
 
     taps_t, taps_h = w.shape[:2]
+
+    def tap(kt, kh, low, high):
+        def plane(k):
+            at = pl.ds(k * (rows + 2) + kh, rows)
+            return x3[low + kt : high + kt, at].reshape((high - low) * rows * width, ch)
+
+        acc[low * rows * width : high * rows * width, :part] += sum(dot_t(plane(k), w[kt, kh, k]) for k in range(3))
+
     fetch.wait()
-    lax.fori_loop(0, taps_h, lambda i, _: (tap(taps_t - 1, i), 0)[1], 0)
+    run_taps(tap, taps_t, taps_h, frames, True)
     spread.wait_recv()
     for row in range(rows + 2):
         inside = True if 0 < row <= rows else (here.up if row == 0 else here.down)
@@ -212,14 +224,11 @@
             @pl.when(jnp.logical_not(inside))
             def _():
                 for f in range(frames):
-                    x3[f, row] = jnp.zeros((width, 3 * ch), BF)
-
-    def rest(i, _):
-        tap(i // taps_h, i % taps_h)
-        return 0
-
-    lax.fori_loop(0, (taps_t - 1) * taps_h, rest, 0)
-    result = acc[...].astype(BF).reshape(frames, rows, width, part)
+                    for k in range(3):
+                        x3[f, k * (rows + 2) + row] = jnp.zeros((width, ch), BF)
+
+    run_taps(tap, taps_t, taps_h, frames, False)
+    result = acc[: frames * rows * width, :part].astype(BF).reshape(frames, rows, width, part)
     halfs[0] = jnp.where(c == 0, result[:, 1].astype(F32), result[:, 0].astype(F32)).astype(BF)
     swap = remote(halfs.at[0], halfs.at[1], es, er, {"chan": 1 - c})
     swap.start()
@@ -236,12 +245,9 @@
     pl.when(here.down)(lambda: to_down.wait_send())
 
 
-def attn_kernel(mine, attn_in, wqkv, wproj, out, every, scores, values, query, send, recv):
-    here = Place()
+def attn_part(here, later, mine, attn_in, wqkv, wproj, out, every, scores, values, query, send, recv):
     frames, width, ch = attn_in.shape
     z, c, chips = here.z, here.c, here.rows
-    here.greet(False, False)
-
     def copy(src, row, f, kind, target):
         return remote(src, every.at[row, f], send.at[row, f, kind], recv.at[row, f], target)
 
@@ -272,6 +278,7 @@
 
     for f in range(frames):
         other(2 * z + 1 - c, f)
+    later()
 
     def hop(k, _):
         sides = ((z - k, z - k >= 0, links[0]), (z + k, z + k < chips, links[1]))
@@ -381,12 +388,11 @@
         pl.when(here.up)(lambda: self.high[0].wait_recv())
 
 
-def last_kernel(
-    second, cache, gain, wup, wlow_hbm, out,
-    wlow, own, stage, prior, chalo, wfull, wmix, wtap, grid, x, upper, acc,
+def last_part(
+    here, second, cache, gain, wup, wlow_hbm, out, x, acc,
+    wlow, own, stage, prior, chalo, wfull, wmix, wtap, grid, upper,
     ss, sr, xs, xr, ps, pr, cs, cr, ws, wr, ls, fs, es, er, us, ur,
 ):
-    here = Place()
     frames, width, ch = second.shape
     c, z = here.c, here.z
     tall = cache.shape[1]
@@ -399,7 +405,6 @@
     fetch.start()
     local = pltpu.make_async_copy(wup, wfull.at[c], ls)
     local.start()
-    here.greet(True, True)
     across = remote(second, stage, xs, xr, {"segment": here.s + 1})
     spread = Deal(here, second, own, ss, sr)
     relay = Deal(here, stage, prior, ps, pr)
@@ -407,12 +412,8 @@
     to_down = remote(cache.at[:, tall - 1], chalo.at[0], cs.at[1], cr.at[1], {"rows": z + 1})
     weights = remote(wup, wfull.at[c], ws, wr, {"chan": 1 - c})
 
-    pl.when(here.has_next)(lambda: across.start())
-    spread.start()
     weights.start()
-    pl.when(first & here.up)(lambda: to_up.start())
-    pl.when(first & here.down)(lambda: to_down.start())
-
+    yield
     for edge, inside in ((0, here.up), (own.shape[0] - 1, here.down)):
 
         @pl.when(jnp.logical_not(inside))
@@ -443,6 +444,11 @@
                     start = side * low + half * part
                     wmix[kh, at, start : start + part] = wfull[half, kh, kw]
 
+    yield
+    pl.when(here.has_next)(lambda: across.start())
+    spread.start()
+    pl.when(first & here.up)(lambda: to_up.start())
+    pl.when(first & here.down)(lambda: to_down.start())
     spread.wait_recv()
 
     @pl.when(here.has_prev)
@@ -462,16 +468,16 @@
         return jnp.where(evens, keep_first(v_prev, v_next), keep_last(v_prev, v_next))
 
     def beside(slot, row, v):
-        x[slot, row, :, two:] = spaced(v, lambda p, n: n, lambda p, n: p).astype(BF)
+        x[slot, tall + 2 + row] = spaced(v, lambda p, n: n, lambda p, n: p).astype(BF)
 
     def put(slot, row, v):
-        x[slot, row, :, :two] = v.astype(BF)
+        x[slot, row] = v.astype(BF)
         beside(slot, row, v)
 
     height = own.shape[0]
 
     def row_copy(slot, at, r):
-        piece = x.at[slot, r, :, pl.ds(0, two)]
+        piece = x.at[slot, r]
         return remote(piece, piece, es.at[at, r], er.at[at, r], {"chan": 1 - c})
 
     def upper_copy(f, r):
@@ -482,14 +488,16 @@
         for kh in range(3):
             n0, n1 = (0, height - 1) if kh == 0 else (0, height) if kh == 1 else (1, height)
             flat = tile[n0:n1].reshape((n1 - n0) * width, ch)
-            grid[kh, n0:n1, :, :two] = (dot_t(flat, wmix[kh, 0]) + dot_t(flat, wmix[kh, 1])).reshape(
+            g0 = sum((height - 1, height)[:kh])
+            g1 = g0 + n1 - n0
+            grid[g0:g1, :, :two] = (dot_t(flat, wmix[kh, 0]) + dot_t(flat, wmix[kh, 1])).reshape(
                 n1 - n0, width, two
             )
-            grid[kh, n0:n1, :, two:] = dot_t(flat, wmix[kh, 2]).reshape(n1 - n0, width, two)
+            grid[g0:g1, :, two:] = dot_t(flat, wmix[kh, 2]).reshape(n1 - n0, width, two)
         for r in range(tall + 2):
             i, odd = (r + 1) // 2, (r + 1) % 2
             sources = (i, i, i + 1) if odd else (i - 1, i, i)
-            both = sum(grid[kh, sources[kh]] for kh in range(3))
+            both = grid[sources[0]] + grid[height - 1 + sources[1]] + grid[2 * height - 2 + sources[2]]
             v = both[:, :two] + spaced(both[:, two:], lambda p, n: p, lambda p, n: n)
             v = v.astype(BF)
             if at and 0 < r <= tall:
@@ -510,16 +518,20 @@
         other = at * frames + 1 - c
         for r in range(tall + 2):
             row_copy(other, at, r).wait_recv()
-            beside(other, r, x[other, r, :, :two].astype(F32))
+            beside(other, r, x[other, r].astype(F32))
 
     raise_frame(own, 1)
     acc[...] = jnp.zeros(acc.shape, F32)
 
-    def tap(kt, kh):
-        v = x[pl.ds(kt, frames), pl.ds(kh, tall)].reshape(frames * tall * width, 2 * two)
-        acc[...] += dot(v, wtap[kt, kh])
-
-    lax.fori_loop(0, taps_h, lambda i, _: (tap(taps_t - 1, i), 0)[1], 0)
+    def tap(kt, kh, low, high):
+        def plane(k):
+            at = pl.ds(k * (tall + 2) + kh, tall)
+            return x[low + kt : high + kt, at].reshape((high - low) * tall * width, two)
+
+        v = jnp.concatenate([plane(0), plane(1)], axis=1)
+        acc[low * tall * width : high * tall * width] += dot(v, wtap[kt, kh])
+
+    run_taps(tap, taps_t, taps_h, frames, True)
 
     @pl.when(here.has_prev)
     def _():
@@ -552,11 +564,7 @@
             for f in range(frames):
                 put(f, row, jnp.zeros((width, two), F32))
 
-    def rest(i, _):
-        tap(i // taps_h, i % taps_h)
-        return 0
-
-    lax.fori_loop(0, (taps_t - 1) * taps_h, rest, 0)
+    run_taps(tap, taps_t, taps_h, frames, False)
     n = 2 * part
     pick = picker(two, n, lambda k, j: k == jnp.where(j < part, j, j - part + low) + c * part)
     for r in range(tall):
@@ -585,6 +593,34 @@
     pl.when(here.has_next)(lambda: across.wait_send())
     pl.when(first & here.up)(lambda: to_up.wait_send())
     pl.when(first & here.down)(lambda: to_down.wait_send())
+
+
+def whole_kernel(counts, *refs):
+    groups = []
+    for count in counts:
+        groups.append(refs[:count])
+        refs = refs[count:]
+    ins, (out,), shared, first, attn, last = groups
+    latent, cache_mid, cache_low, gain_mid, gain_attn, gain_low, conv_mid, attn_qkv, attn_proj, conv_up, conv_low = ins
+    mine, attn_in, second, wqkv, wproj, low_cache, sems, x, acc = shared
+    fetches = [
+        pltpu.make_async_copy(src, dst, sems.at[i])
+        for i, (src, dst) in enumerate(((attn_qkv, wqkv), (attn_proj, wproj), (cache_low, low_cache)))
+    ]
+    here = Place()
+    here.greet(True, True)
+    tail = last_part(here, second, low_cache, gain_low, conv_up, conv_low, out, x, acc, *last)
+    first_part(here, latent, cache_mid, gain_mid, gain_attn, conv_mid, mine, attn_in, *first, lambda: start(tail, fetches), x, acc)
+    for fetch in fetches:
+        fetch.wait()
+    attn_part(here, lambda: next(tail), mine, attn_in, wqkv, wproj, second, *attn)
+    next(tail, None)
+
+
+def start(tail, fetches):
+    for fetch in fetches:
+        fetch.start()
+    next(tail)
 
 
 def call(kernel, number, outs, scratch, *args, far=()):
@@ -595,7 +631,7 @@
         out_specs=jax.tree.map(lambda _: pl.BlockSpec(memory_space=pltpu.VMEM), outs),
         scratch_shapes=scratch,
         compiler_params=pltpu.CompilerParams(
-            collective_id=number, has_side_effects=True, vmem_limit_bytes=60 * 1024 * 1024
+            collective_id=number, has_side_effects=True, vmem_limit_bytes=67043328
         ),
     )(*args)
 
@@ -608,53 +644,35 @@
     dma, one = pltpu.SemaphoreType.DMA, pltpu.SemaphoreType.DMA(())
     row = jax.ShapeDtypeStruct((frames, width, ch), BF)
     taps_t, taps_h, taps_w = conv_mid.shape[:3]
-    mine, attn_in = call(
-        first_kernel,
-        0,
-        (row, row),
-        [
+    total = rows * lax.axis_size("rows")
+    vm = pltpu.VMEM(row.shape, BF)
+    cache_t = jnp.swapaxes(cache_low, 2, 3)
+    shared = [
+        vm, vm, vm, pltpu.VMEM(attn_qkv.shape, BF), pltpu.VMEM(attn_proj.shape, BF), pltpu.VMEM(cache_t.shape, BF),
+        dma((3,)),
+        pltpu.VMEM((2 * frames, max(taps_w * (rows + 2), 2 * (cache_low.shape[1] + 2)), width, ch), BF),
+        pltpu.VMEM((frames * cache_low.shape[1] * width, 2 * conv_low.shape[-1]), F32),
+    ]
+    first = [
             pltpu.VMEM((taps_t, taps_h, taps_w, part, ch), BF),
             pltpu.VMEM((2, frames, width, ch), BF),
             pltpu.VMEM((rows + 2, frames, width, ch), BF),
-            pltpu.VMEM((2 * frames, rows + 2, width, taps_w * ch), BF),
-            pltpu.VMEM((frames * rows * width, part), F32),
             pltpu.VMEM((2, frames, width, part), BF),
             dma((2,)), dma((2,)), one, one, dma((3,)), dma((3,)), one, one, one, one,
-        ],
-        latent,
-        cache_mid,
-        gain_mid,
-        gain_attn,
-        jnp.swapaxes(conv_mid, 3, 4),
-        far=(4,),
-    )
-    total = rows * lax.axis_size("rows")
-    second = call(
-        attn_kernel,
-        1,
-        row,
-        [
+    ]
+    attn = [
             pltpu.VMEM((total, frames, width, ch), BF),
             pltpu.VMEM((total, frames, width, width), F32),
             pltpu.VMEM((total, frames, width, ch), BF),
             pltpu.VMEM((frames, width, ch), BF),
             dma((total, frames, 3)),
             dma((total, frames)),
-        ],
-        mine,
-        attn_in,
-        attn_qkv,
-        attn_proj,
-    )
+    ]
     _, tall, wide, low = cache_low.shape
     cut = conv_low.shape[-1]
     two = 2 * low
     taps_t, taps_h, taps_w = conv_low.shape[:3]
-    decoded = call(
-        last_kernel,
-        2,
-        jax.ShapeDtypeStruct((frames, tall, cut, wide), BF),
-        [
+    last = [
             pltpu.VMEM((taps_t, taps_h, taps_w * low, cut), BF),
             pltpu.VMEM((rows + 2, width, ch), BF),
             pltpu.VMEM((frames, width, ch), BF),
@@ -663,19 +681,23 @@
             pltpu.VMEM((2, 3, 3, cut, ch), BF),
             pltpu.VMEM((3, 3, two, ch), BF),
             pltpu.VMEM((taps_t, taps_h, 2 * two, 2 * cut), BF),
-            pltpu.VMEM((3, rows + 2, width, 2 * two), F32),
-            pltpu.VMEM((2 * frames, tall + 2, width, 2 * two), BF),
+            pltpu.VMEM((3 * rows + 4, width, 2 * two), F32),
             pltpu.VMEM((frames, tall, width, two), BF),
-            pltpu.VMEM((frames * tall * width, 2 * cut), F32),
             dma((4,)), dma((3,)), one, one, dma((4,)), dma((3,)), dma((2,)), dma((2,)), one, one, one, one,
             dma((2, tall + 2)), dma((2, tall + 2)), dma((tall,)), dma((tall,)),
-        ],
-        second,
-        jnp.swapaxes(cache_low, 2, 3),
-        gain_low,
-        jnp.swapaxes(conv_up, 2, 3),
-        conv_low.reshape(taps_t, taps_h, taps_w * low, cut),
-        far=(4,),
+    ]
+    args = (
+        latent, cache_mid, cache_t, gain_mid, gain_attn, gain_low, jnp.swapaxes(conv_mid, 3, 4), attn_qkv, attn_proj,
+        jnp.swapaxes(conv_up, 2, 3), conv_low.reshape(taps_t, taps_h, taps_w * low, cut),
+    )
+    counts = (len(args), 1, len(shared), len(first), len(attn), len(last))
+    decoded = call(
+        functools.partial(whole_kernel, counts),
+        0,
+        jax.ShapeDtypeStruct((frames, tall, cut, wide), BF),
+        shared + first + attn + last,
+        *args,
+        far=(2, 6, 7, 8, 10),
     )
     return jnp.swapaxes(decoded, 2, 3)
 

time: 83.6 us -> 74.6 us (0.89)
  Pallas kernels: 81.4 us -> 72 us
    pallas_call x3 -> x1, Pallas kernels: 81.4 us -> 72 us  [call(): pl.pallas_call(kernel, out_shape=outs, in_specs=[pl.BlockSpec(memory_spac...]
where the time goes in v2:
time: 74.6 us; the launch traced here: 73.9 us
  Pallas kernels  72 us (97%)
  local copies, waits for them, and re-layouts  1.94 us (3%)
    pallas_call x1, Pallas kernels, call(): pl.pallas_call(kernel, out_shape=outs, in_specs=[pl.BlockSpec(memory_spac...  72 us
    unnamed x1, local copies, waits for them, and re-layouts  1.94 us

profile of v2, /device:TPU:2, one launch (start us, length us, event | category | flops | bytes accessed | tf_op | source)
XLA Modules:
  0.0 73.9 jit_solution(13822808683808856520)
XLA Ops:
  0.0 72.0 %shard_map.109 = bf16[2,4,96,320]{3,2,1,0:T(8,128)(2,1)} custom-call(bf16[2,2,160,384]{3,2,1,0:T(8,128)(2,1)} %refs_0_.1, bf16[2,2,160,384]{3,2,1,0:T(8,128)(2,1)} %refs_1_.1, bf16[2,4,192,320]{3,2,1,0:T(8,128)(2,1)} %bitcast.8, f32[384]{0:T(512)} %refs_3_.1, f32[384]{0:T(512)} %refs_4_.1, f32[192]{0:T(256)} %refs_5_.1, ...), custom_call_target="tpu_custom_call" | custom-call | tf_op jit(solution)/shard_map/pallas_call | solution.py:627
  72.0 1.9 %copy.13 = bf16[2,4,320,96]{2,3,1,0:T(8,128)(2,1)} copy(bf16[2,4,320,96]{2,3,1,0:T(8,128)(2,1)} %bitcast.6) | data formatting | bytes 983040
